TPU v7x, 256 devices: a whole 4x4x8 slice. The times are simulated.
256 devices in a mesh: seq: 32 (over x, z), head: 8 (over y, core).
Axes of the slice: x: 4, y: 4, z: 8, core: 2. Of those that a mesh axis runs over, the one named last changes fastest.
Arguments:
- queries: bfloat16 [32768, 5120], P('seq', 'head')
- keys: bfloat16 [32768, 5120], P('seq', 'head')
- values: bfloat16 [32768, 5120], P('seq', 'head'), may hold values from -6 to 6
- query_gain: float32 [5120], P('head'), may hold values from 0.1 to 1.9
- key_gain: float32 [5120], P('head'), may hold values from 0.1 to 1.9
- shapes: int32 [8, 3], replicated, may hold values from 4 to 32, as said below
- windows: int32 [256, 27], P('seq'), may hold values from -1 to 255, as said below
- text_keys: bfloat16 [32, 256, 5120], P(None, 'seq', 'head')
- text_values: bfloat16 [32, 256, 5120], P(None, 'seq', 'head'), may hold values from -6 to 6
- owner: int32 [8], replicated, may hold values from 0 to 31, as said below
Outputs:
- attended: bfloat16 [32768, 5120], P('seq', 'head')
Inputs may be any that keep to these rules, and one draw needn't show every extreme that they name: `shapes`: row s is (frames, height, width) of video s in tokens: height and width are 16 and 32, or 32 and 16, so a frame has 4 tiles; each video has from 16 to 48 tiles, and the videos' tiles add up to 256, so no tile holds tokens of two videos. `windows`: entry k of row g stands for the tile k // 9 - 1 frames, (k // 3) % 3 - 1 tile rows and k % 3 - 1 tile columns away from tile g in its video: it holds that tile's number or -1; it is -1 wherever that tile lies outside the video, and entry 13 is always g. `owner`: no two videos share a panel.
All inputs are finite; a program needn't handle non-finite values.
Results may differ from a plain program's by a relative error of at most 0.012.
Values may be sent and summed in bfloat16 or wider, within the bound.
A program may use at most 128 MiB of HBM per device.

v0:
```python
import jax
import jax.numpy as jnp
from jax import lax
from jax.sharding import PartitionSpec as P

HEAD_DIM = 128
D = 5120
TILE_H = 8
TILE_W = 16
REACH = 7
TXT = 256
epsilon = 1e-06


def extended_2(cells, sides, width):
    for axis, dim in sides:
        count = lax.axis_size(axis)
        ends = count - 1
        head = lax.slice_in_dim(cells, 0, width, axis=dim)
        tail = lax.slice_in_dim(cells, cells.shape[dim] - width, cells.shape[dim], axis=dim)
        cells = jnp.concatenate(
            [
                lax.ppermute(tail, axis, [(i, (i + 1) % count) for i in range(ends)]),
                cells,
                lax.ppermute(head, axis, [((i + 1) % count, i) for i in range(ends)]),
            ],
            axis=dim,
        )
    return cells


def tile_table(shape_rows):
    per_frame = shape_rows[:, 1] // TILE_H * (shape_rows[:, 2] // TILE_W)
    tile_counts = shape_rows[:, 0] * per_frame
    tile_ends = jnp.cumsum(tile_counts)
    return (tile_ends - tile_counts, tile_ends)


def locate(tile_ids, shape_rows, tile_starts, tile_ends):
    sample_ids = jnp.sum((tile_ids[:, None] >= tile_ends[None, :]).astype(jnp.int32), axis=1)
    one_hot = (
        sample_ids[:, None] == jnp.arange(tile_ends.shape[0], dtype=jnp.int32)[None, :]
    ).astype(jnp.int32)
    first_tiles = jnp.sum(one_hot * tile_starts[None, :], axis=1)
    row_counts = jnp.sum(one_hot * (shape_rows[:, 1] // TILE_H)[None, :], axis=1)
    col_counts = jnp.sum(one_hot * (shape_rows[:, 2] // TILE_W)[None, :], axis=1)
    offsets = tile_ids - first_tiles
    per_frame = row_counts * col_counts
    within = offsets % per_frame
    return (sample_ids, one_hot, offsets // per_frame, within // col_counts, within % col_counts)


def rope_angles(frames, bands, columns, head_size):
    inner = jnp.arange(TILE_H * TILE_W, dtype=jnp.int32)
    tile_total = frames.shape[0]
    time_pos = (
        jnp.broadcast_to(frames[:, None], (tile_total, inner.shape[0]))
        .reshape(-1)
        .astype(jnp.float32)
    )
    row_pos = (bands[:, None] * TILE_H + inner[None, :] // TILE_W).reshape(-1).astype(jnp.float32)
    col_pos = (columns[:, None] * TILE_W + inner[None, :] % TILE_W).reshape(-1).astype(jnp.float32)
    third = head_size // 6
    part_sizes = (head_size - 4 * third, 2 * third, 2 * third)
    angle_parts = []
    for position, part_size in zip((time_pos, row_pos, col_pos), part_sizes):
        frequency = 10000.0 ** (-jnp.arange(0, part_size, 2, dtype=jnp.float32) / part_size)
        angle_parts.append(position[:, None] * frequency[None, :])
    return jnp.concatenate(angle_parts, axis=1)


def rotate(field, angles):
    paired = field.reshape(field.shape[0], field.shape[1], field.shape[2] // 2, 2)
    cosine = jnp.cos(angles)[:, None, :]
    sine = jnp.sin(angles)[:, None, :]
    even_part = paired[..., 0]
    odd_part = paired[..., 1]
    turned = jnp.stack(
        [even_part * cosine - odd_part * sine, even_part * sine + odd_part * cosine], axis=-1
    )
    return turned.reshape(field.shape)


def finish_rows(widened, squares, gain, angles, head_count):
    scaled = widened * lax.rsqrt(squares / D + epsilon)[:, None] * gain[None, :]
    turned = rotate(scaled.reshape(widened.shape[0], head_count, HEAD_DIM), angles)
    return turned.reshape(widened.shape).astype(jnp.bfloat16)


def local(
    queries, keys, values, query_gain, key_gain, shapes, windows, text_keys, text_values, owner
):
    row_count, feat_width = queries.shape
    head_count = feat_width // HEAD_DIM
    tile_rows = TILE_H * TILE_W
    tiles_here = row_count // tile_rows
    first_global = lax.axis_index("seq") * tiles_here
    tile_starts, tile_ends = tile_table(shapes)
    tile_ids = first_global + jnp.arange(tiles_here, dtype=jnp.int32)
    sample_ids, one_hot, frames, bands, columns = locate(tile_ids, shapes, tile_starts, tile_ends)
    angles = rope_angles(frames, bands, columns, HEAD_DIM)
    query_wide = queries.astype(jnp.float32)
    key_wide = keys.astype(jnp.float32)
    query_squares, key_squares = lax.psum(
        (jnp.sum(query_wide * query_wide, axis=1), jnp.sum(key_wide * key_wide, axis=1)), "head"
    )
    q_hat = finish_rows(query_wide, query_squares, query_gain, angles, head_count)
    k_hat = finish_rows(key_wide, key_squares, key_gain, angles, head_count)
    key_value = jnp.stack([k_hat, values])
    extended = extended_2(key_value, (("seq", 1),), REACH * tile_rows)
    panel_of_tile = jnp.sum(one_hot * owner[None, :], axis=1)
    prompt_pair = jnp.stack([text_keys, text_values])
    every_panel = lax.all_gather(prompt_pair, "seq", axis=2, tiled=True)
    wanted = jnp.stack([panel_of_tile[0], panel_of_tile[tiles_here - 1]])
    panels = jnp.take(every_panel, wanted, axis=1)
    prompt_keys = panels[0].reshape(2 * TXT, head_count, HEAD_DIM)
    prompt_values = panels[1].reshape(2 * TXT, head_count, HEAD_DIM)
    second_slot = (sample_ids != sample_ids[0]).astype(jnp.int32)
    prompt_allowed = second_slot[:, None] == (jnp.arange(2 * TXT, dtype=jnp.int32) // TXT)[None, :]
    key_tiles = first_global - REACH + jnp.arange(tiles_here + 2 * REACH, dtype=jnp.int32)
    window_allowed = (
        jnp.any(windows[:, :, None] == key_tiles[None, None, :], axis=1) & (key_tiles >= 0)[None, :]
    )
    group_tiles = 4
    span_tiles = group_tiles + 2 * REACH
    group_rows = group_tiles * tile_rows
    factor = HEAD_DIM ** (-0.5)

    def attend(block_index):
        start_tile = block_index * group_tiles
        query_rows = lax.dynamic_slice_in_dim(q_hat, start_tile * tile_rows, group_rows, 0).reshape(
            group_rows, head_count, HEAD_DIM
        )
        key_rows = lax.dynamic_slice_in_dim(
            extended[0], start_tile * tile_rows, span_tiles * tile_rows, 0
        ).reshape(span_tiles * tile_rows, head_count, HEAD_DIM)
        value_rows = lax.dynamic_slice_in_dim(
            extended[1], start_tile * tile_rows, span_tiles * tile_rows, 0
        ).reshape(span_tiles * tile_rows, head_count, HEAD_DIM)
        allowed = lax.dynamic_slice(
            window_allowed, (start_tile, start_tile), (group_tiles, span_tiles)
        )
        prompt_ok = lax.dynamic_slice_in_dim(prompt_allowed, start_tile, group_tiles, 0)
        key_mask = jnp.concatenate(
            [
                jnp.repeat(jnp.repeat(allowed, tile_rows, axis=0), tile_rows, axis=1),
                jnp.repeat(prompt_ok, tile_rows, axis=0),
            ],
            axis=1,
        )
        all_keys = jnp.concatenate([key_rows, prompt_keys], axis=0)
        all_values = jnp.concatenate([value_rows, prompt_values], axis=0)
        scores = (
            jnp.einsum("qhd,khd->hqk", query_rows, all_keys, preferred_element_type=jnp.float32)
            * factor
        )
        scores = jnp.where(key_mask[None, :, :], scores, -jnp.inf)
        largest = jnp.max(scores, axis=-1, keepdims=True)
        weights = jnp.exp(scores - largest)
        totals = jnp.sum(weights, axis=-1)
        mixed = jnp.einsum(
            "hqk,khd->qhd",
            weights.astype(jnp.bfloat16),
            all_values,
            preferred_element_type=jnp.float32,
        )
        mixed = mixed / jnp.transpose(totals)[:, :, None]
        return mixed.astype(jnp.bfloat16).reshape(group_rows, feat_width)

    outputs = lax.map(attend, jnp.arange(tiles_here // group_tiles, dtype=jnp.int32))
    return outputs.reshape(row_count, feat_width)


def solution(mesh):
    placed = (
        P("seq", "head"),
        P("seq", "head"),
        P("seq", "head"),
        P("head"),
        P("head"),
        P(),
        P("seq", None),
        P(None, "seq", "head"),
        P(None, "seq", "head"),
        P(),
    )
    return jax.shard_map(
        local, mesh=mesh, in_specs=placed, out_specs=P("seq", "head"), check_vma=False
    )
```

profile of v0, /device:TPU:1, one launch (start us, length us, event | category | flops | bytes accessed | tf_op | source)
XLA Modules:
  0.0 366.4 jit_solution(5512880522823748688)
XLA Ops:
  9.4 15.2 %all-reduce = (f32[1024]{0:T(1024)S(1)}, f32[1024]{0:T(1024)S(1)}) all-reduce(f32[1024]{0:T(1024)S(1)} %fusion.26, f32[1024]{0:T(1024)S(1)} %fusion.28), channel_id=1, replica_groups=mesh['seq'=32,'head'=8] {'head'}, use_global_device_ids=true, to_apply=%region_8.9 | all-reduce | flops 2048 | bytes 16384 | tf_op jit(solution)/shard_map/psum | solution.py:104
  28.4 4.5 %reshape_reshape.8 = f32[1024,5,64,2]{0,3,2,1:T(2,128)} reshape(f32[1024,640]{0,1:T(8,128)} %copy.28) | data formatting | bytes 5242880 | tf_op jit(solution)/shard_map/reshape;reshape | solution.py:73
  36.7 4.6 %reshape_reshape.9 = f32[1024,5,64,2]{0,3,2,1:T(2,128)} reshape(f32[1024,640]{0,1:T(8,128)} %copy.31) | data formatting | bytes 5242880 | tf_op jit(solution)/shard_map/reshape;reshape | solution.py:73
  43.7 9.1 %subtract_convert_fusion = (bf16[1024,5,64,1]{0,3,2,1:T(2,128)(2,1)}, bf16[1024,5,64,1]{0,3,2,1:T(2,128)(2,1)}, bf16[1024,5,64,1]{0,3,2,1:T(2,128)(2,1)S(1)}, bf16[1024,5,64,1]{0,3,2,1:T(2,128)(2,1)S(1)}) fusion(f32[1024,5,64,2]{0,3,2,1:T(2,128)} %reshape_reshape.9, f32[1024,64]{0,1:T(8,128)S(1)} %get-tuple-element.183, ...), kind=kLoop, calls=%fused_computation.46 | loop fusion | flops 5242880 | bytes 8388608 | tf_op jit(solution)/shard_map/convert.2
  60.4 3.5 collective-permute-start
  65.3 5.8 %pad_maximum_fusion.3 = bf16[1024,5,64,2]{0,3,2,1:T(2,128)(2,1)} fusion(bf16[1024,5,64,1]{0,3,2,1:T(2,128)(2,1)} %get-tuple-element.173, bf16[1024,5,64,1]{0,3,2,1:T(2,128)(2,1)} %get-tuple-element.172), kind=kLoop, calls=%fused_computation.43 | loop fusion | flops 2621440 | bytes 2621440 | tf_op jit(solution)/shard_map/stack | solution.py:78
  71.1 4.1 %convert_element_type.86 = bf16[1024,640]{0,1:T(8,128)(2,1)} reshape(bf16[1024,5,64,2]{0,3,2,1:T(2,128)(2,1)} %pad_maximum_fusion.3) | data formatting | bytes 2621440 | tf_op jit(solution)/shard_map/convert_element_type | solution.py:87
  79.3 69.1 %collective-permute-done = bf16[2,896,640]{1,2,0:T(8,128)(2,1)} collective-permute-done((bf16[2,896,640]{1,2,0:T(8,128)(2,1)}, bf16[2,896,640]{1,2,0:T(8,128)(2,1)}, u32[]{:S(2)}, u32[]{:S(2)}) %collective-permute-start) | collective-permute-done | bytes 2293792 | tf_op jit(solution)/shard_map/ppermute | solution.py:23
  148.4 10.5 %collective-permute-done.1 = bf16[2,896,640]{1,2,0:T(8,128)(2,1)} collective-permute-done((bf16[2,896,640]{1,2,0:T(8,128)(2,1)}, bf16[2,896,640]{1,2,0:T(8,128)(2,1)}, u32[]{:S(2)}, u32[]{:S(2)}) %collective-permute-start.1) | collective-permute-done | bytes 2293792 | tf_op jit(solution)/shard_map/ppermute | solution.py:25
  158.9 5.7 %pad_maximum_fusion = bf16[2,2816,640]{1,2,0:T(8,128)(2,1)} fusion(bf16[2,896,640]{1,2,0:T(8,128)(2,1)} %collective-permute-done.1, bf16[1,1024,640]{1,2,0:T(8,128)(2,1)S(1)} %bitcast.119, bf16[1,1024,640]{1,2,0:T(8,128)(2,1)S(1)} %convert_element_type.83, bf16[2,896,640]{1,2,0:T(8,128)(2,1)} %collective-permute-done), kind=kLoop, calls=%fused_computation.29 | loop fusion | flops 28835840 | bytes 14417920 | tf_op jit(solution)/shard_map/concatenate | solution.py:21
  164.7 57.8 %all-gather.2.cloned.1.call-done = bf16[2,32,256,640]{3,2,1,0:T(8,128)(2,1)} async-done(((bf16[2,32,8,640]{3,2,1,0:T(8,128)(2,1)}), bf16[2,32,256,640]{3,2,1,0:T(8,128)(2,1)}) %all-gather.2.cloned.1.call-update) | async-done | bytes 20971536 | tf_op jit(solution)/shard_map/all_gather | solution.py:113
  222.5 7.7 %gather_fusion = bf16[2,2,256,640]{3,2,1,0:T(8,128)(2,1)S(1)} fusion(bf16[2,32,256,640]{3,2,1,0:T(8,128)(2,1)} %all-gather.2.cloned.1.call-done, s32[1024]{0:T(1024)S(1)} %pad_clamp_fusion), kind=kCustom, calls=%fused_computation | custom fusion | bytes 2621448 | tf_op jit(solution)/shard_map/jit(_take)/gather | solution.py:115
  234.4 125.1 %while.12 = (s32[]{:T(128)}, bf16[2,512,640]{2,1,0:T(8,128)(2,1)}, bf16[2,2816,640]{1,2,0:T(8,128)(2,1)}, s32[2]{0:T(128)S(1)}, bf16[512,5,128]{0,2,1:T(8,128)(2...) while((s32[]{:T(128)}, bf16[2,512,640]{2,1,0:T(8,128)(2,1)}, ...), condition=%wide.region_14.15_spmd, body=%wide.region_11.14_spmd.sunk | while | flops 3786796032 | bytes 151642208 | solution.py:170
  238.7 3.2 copy.51
  242.7 3.6 fusion.54
  248.3 3.3 copy.52
  252.8 15.2 %fusion.55 = (f32[5,512]{1,0:T(8,128)S(1)}, f32[5,512,2816]{2,1,0:T(8,128)}) fusion(pred[512,2816]{1,0:T(8,128)(4,1)} %copy.51, bf16[512,5,128]{0,2,1:T(8,128)(2,1)S(1)} %bitcast.117, bf16[512,5,128]{2,0,1:T(8,128)(2,1)} %get-tuple-element.304, bf16[2304,5,128]{2,0,1:T(8,128)(2,1)} %copy.52), kind=kOutput, calls=%fused_computation.3.clone.1 | convolution fusion | flops 1874327040 | bytes 34547712 | tf_op jit(solution)/shard_map/while/body/eval_jaxpr/qhd,khd->hqk/dot_general | solution.py:154
  268.0 13.8 %fusion.56 = f32[5,512]{1,0:T(8,128)S(1)} fusion(f32[5,512,2816]{2,1,0:T(8,128)} %get-tuple-element.257, f32[5,512]{1,0:T(8,128)S(1)} %get-tuple-element.258, pred[512,2816]{1,0:T(8,128)(4,1)S(1)} %copy-done), kind=kLoop, calls=%fused_computation.4.clone.1 | loop fusion | flops 28833280 | bytes 30298112 | tf_op jit(solution)/shard_map/while/body/eval_jaxpr/reduce_sum | solution.py:160
  281.7 14.1 %divide_convert_fusion.2 = bf16[512,5,128]{0,2,1:T(8,128)(2,1)S(1)} fusion(f32[512,5]{0,1:T(8,128)S(1)} %bitcast.122, f32[5,512,2816]{2,1,0:T(8,128)} %get-tuple-element.257, f32[5,512]{1,0:T(8,128)S(1)} %get-tuple-element.258, pred[512,2816]{1,0:T(8,128)(4,1)S(1)} %copy-done, bf16[512,5,128]{0,2,1:T(8,128)(2,1)S(1)} %copy-done.4, ...), kind=kOutput, calls=%fused_computation.17.clone.1 | convolution fusion | flops 1882193920 | bytes 34557952 | tf_op jit(solution)/shard_map/while/body/eval_jaxpr/hqk,khd->qhd/dot_general | solution.py:161
  305.2 3.6 fusion.54
  310.9 3.3 copy.52
  315.3 15.2 %fusion.55 = (f32[5,512]{1,0:T(8,128)S(1)}, f32[5,512,2816]{2,1,0:T(8,128)}) fusion(pred[512,2816]{1,0:T(8,128)(4,1)} %copy.51, bf16[512,5,128]{0,2,1:T(8,128)(2,1)S(1)} %bitcast.117, bf16[512,5,128]{2,0,1:T(8,128)(2,1)} %get-tuple-element.304, bf16[2304,5,128]{2,0,1:T(8,128)(2,1)} %copy.52), kind=kOutput, calls=%fused_computation.3.clone.1 | convolution fusion | flops 1874327040 | bytes 34547712 | tf_op jit(solution)/shard_map/while/body/eval_jaxpr/qhd,khd->hqk/dot_general | solution.py:154
  330.5 13.8 %fusion.56 = f32[5,512]{1,0:T(8,128)S(1)} fusion(f32[5,512,2816]{2,1,0:T(8,128)} %get-tuple-element.257, f32[5,512]{1,0:T(8,128)S(1)} %get-tuple-element.258, pred[512,2816]{1,0:T(8,128)(4,1)S(1)} %copy-done), kind=kLoop, calls=%fused_computation.4.clone.1 | loop fusion | flops 28833280 | bytes 30298112 | tf_op jit(solution)/shard_map/while/body/eval_jaxpr/reduce_sum | solution.py:160
  344.3 14.1 %divide_convert_fusion.2 = bf16[512,5,128]{0,2,1:T(8,128)(2,1)S(1)} fusion(f32[512,5]{0,1:T(8,128)S(1)} %bitcast.122, f32[5,512,2816]{2,1,0:T(8,128)} %get-tuple-element.257, f32[5,512]{1,0:T(8,128)S(1)} %get-tuple-element.258, pred[512,2816]{1,0:T(8,128)(4,1)S(1)} %copy-done, bf16[512,5,128]{0,2,1:T(8,128)(2,1)S(1)} %copy-done.4, ...), kind=kOutput, calls=%fused_computation.17.clone.1 | convolution fusion | flops 1882193920 | bytes 34557952 | tf_op jit(solution)/shard_map/while/body/eval_jaxpr/hqk,khd->qhd/dot_general | solution.py:161
  (104 shorter events, 49.0 us)
Async XLA Ops:
  6.5 2.2 copy-start.2
  6.5 2.5 copy-start.3
  6.5 18.1 %copy-start.7 = (f32[640]{0:T(1024)S(1)}, f32[640]{0:T(1024)}, u32[]{:S(2)}) copy-start(f32[640]{0:T(1024)} %param.16) | copy-start | bytes 7684
  6.5 215.9 %all-gather.2.cloned.1.call-start = ((), (), s32[]{:S(2)}) async-start(), calls=%async_computation | async-start | bytes 21626880 | tf_op jit(solution)/shard_map/all_gather | solution.py:113
  28.4 4.5 %copy-start.8 = (f32[640]{0:T(1024)S(1)}, f32[640]{0:T(1024)}, u32[]{:S(2)}) copy-start(f32[640]{0:T(1024)} %param.15) | copy-start | bytes 7684
  36.7 4.6 %copy-start.5 = (s32[8,3]{0,1:T(4,128)S(1)}, s32[8,3]{0,1:T(4,128)}, u32[]{:S(2)}) copy-start(s32[8,3]{0,1:T(4,128)} %param.17) | copy-start | bytes 292
  36.7 5.0 %copy-start.9 = (s32[8]{0:T(128)S(1)}, s32[8]{0:T(128)}, u32[]{:S(2)}) copy-start(s32[8]{0:T(128)} %param.21) | copy-start | bytes 100
  36.7 7.0 %copy-start.1 = (f32[1024,5,64,2]{0,3,2,1:T(2,128)S(1)}, f32[1024,5,64,2]{0,3,2,1:T(2,128)}, u32[]{:S(2)}) copy-start(f32[1024,5,64,2]{0,3,2,1:T(2,128)} %reshape_reshape.8) | copy-start | bytes 7864324
  60.4 88.1 %collective-permute-start = (bf16[2,896,640]{1,2,0:T(8,128)(2,1)}, bf16[2,896,640]{1,2,0:T(8,128)(2,1)}, u32[]{:S(2)}, u32[]{:S(2)}) collective-permute-start(bf16[2,896,640]{1,2,0:T(8,128)(2,1)} %get-tuple-element.176), channel_id=1, source_target_pairs={{0,8},{8,16},{16,24},{24,32},{32,40},{40,48},{48,56},{56,64},{64,7... | collective-permute-start | bytes 6881288 | tf_op jit(solution)/shard_map/ppermute | solution.py:23
  63.8 95.1 %collective-permute-start.1 = (bf16[2,896,640]{1,2,0:T(8,128)(2,1)}, bf16[2,896,640]{1,2,0:T(8,128)(2,1)}, u32[]{:S(2)}, u32[]{:S(2)}) collective-permute-start(bf16[2,896,640]{1,2,0:T(8,128)(2,1)} %get-tuple-element.177), channel_id=1, source_target_pairs={{8,0},{16,8},{24,16},{32,24},{40,32},{48,40},{56,48},{64,56},{72,6... | collective-permute-start | bytes 6881288 | tf_op jit(solution)/shard_map/ppermute | solution.py:25
  65.3 13.2 %copy-start.6 = (s32[8,27]{1,0:T(8,128)S(1)}, s32[8,27]{1,0:T(8,128)}, u32[]{:S(2)}) copy-start(s32[8,27]{1,0:T(8,128)} %param.18) | copy-start | bytes 2596
  252.8 15.2 %copy-start = (pred[512,2816]{1,0:T(8,128)(4,1)S(1)}, pred[512,2816]{1,0:T(8,128)(4,1)}, u32[]{:S(2)}) copy-start(pred[512,2816]{1,0:T(8,128)(4,1)} %copy.51) | copy-start | bytes 4325380 | tf_op jit(solution)/shard_map/while
  268.0 13.8 %copy-start.4 = (bf16[512,5,128]{0,2,1:T(8,128)(2,1)S(1)}, bf16[512,5,128]{0,2,1:T(8,128)(2,1)}, u32[]{:S(2)}) copy-start(bf16[512,5,128]{0,2,1:T(8,128)(2,1)} %get-tuple-element.300) | copy-start | bytes 1966084 | tf_op jit(solution)/shard_map/while
  315.3 15.2 %copy-start = (pred[512,2816]{1,0:T(8,128)(4,1)S(1)}, pred[512,2816]{1,0:T(8,128)(4,1)}, u32[]{:S(2)}) copy-start(pred[512,2816]{1,0:T(8,128)(4,1)} %copy.51) | copy-start | bytes 4325380 | tf_op jit(solution)/shard_map/while
  330.5 13.8 %copy-start.4 = (bf16[512,5,128]{0,2,1:T(8,128)(2,1)S(1)}, bf16[512,5,128]{0,2,1:T(8,128)(2,1)}, u32[]{:S(2)}) copy-start(bf16[512,5,128]{0,2,1:T(8,128)(2,1)} %get-tuple-element.300) | copy-start | bytes 1966084 | tf_op jit(solution)/shard_map/while
Sparse Core Ops, SparseCore 0:
  10.0 212.3 all-gather.1
where the time goes:
time: 367 us; the launch traced here: 366 us
  waiting for transfers between devices  137 us (37%)
  local copies, waits for them, and re-layouts  67.2 us (18%)
  other arithmetic  66.6 us (18%)
  matrix products  58.5 us (16%)
  blocking collectives  15.2 us (4%)
  between operations  13.6 us (4%)
  starting transfers between devices  4.92 us (1%)
    ppermute x1, waiting for transfers between devices, extended_2(): lax.ppermute(tail, axis, [(i, (i + 1) % count) for i in range(ends)])  69.1 us
    all_gather x1, waiting for transfers between devices, local(): every_panel = lax.all_gather(prompt_pair, 'seq', axis=2, tiled=True)  57.8 us
    dot_general x2, matrix products, attend(): jnp.einsum('qhd,khd->hqk', query_rows, all_keys, preferred_element_type=j...  30.4 us
    dot_general x2, matrix products, attend(): jnp.einsum('hqk,khd->qhd', weights.astype(jnp.bfloat16), all_values, pref...  28.1 us
    reduce_sum x2, other arithmetic, attend(): totals = jnp.sum(weights, axis=-1)  27.5 us
    psum x1, blocking collectives, local(): lax.psum((jnp.sum(query_wide * query_wide, axis=1), jnp.sum(key_wide * ke...  15.2 us
    ppermute x1, waiting for transfers between devices, extended_2(): lax.ppermute(head, axis, [((i + 1) % count, i) for i in range(ends)])  10.5 us
    another operation x2, other arithmetic  9.31 us
  transfers between devices with their start and end apart: 3, of which 3 were waited for; matrix products, arithmetic and copies ran while one was open for 15% of the time, Pallas kernels for 0%

commit v1 on v0

--- a/solution.py
+++ b/solution.py
@@ -110,7 +110,9 @@
     extended = extended_2(key_value, (("seq", 1),), REACH * tile_rows)
     panel_of_tile = jnp.sum(one_hot * owner[None, :], axis=1)
     prompt_pair = jnp.stack([text_keys, text_values])
-    every_panel = lax.all_gather(prompt_pair, "seq", axis=2, tiled=True)
+    every_panel = jnp.concatenate(
+        lax.all_to_all(jnp.stack([prompt_pair] * lax.axis_size("seq")), "seq", 0, 0), axis=2
+    )
     wanted = jnp.stack([panel_of_tile[0], panel_of_tile[tiles_here - 1]])
     panels = jnp.take(every_panel, wanted, axis=1)
     prompt_keys = panels[0].reshape(2 * TXT, head_count, HEAD_DIM)

time: 367 us -> 741 us (2.02)
  the two profiles are of different devices: /device:TPU:1 before, /device:TPU:103 now
where the time goes in v1:
time: 741 us; the launch traced here: 740 us
  waiting for transfers between devices  489 us (66%)
  local copies, waits for them, and re-layouts  94.4 us (13%)
  other arithmetic  65.3 us (9%)
  matrix products  57.4 us (8%)
  starting transfers between devices  16.4 us (2%)
  blocking collectives  13.8 us (2%)
    ppermute x1, waiting for transfers between devices, extended_2(): lax.ppermute(tail, axis, [(i, (i + 1) % count) for i in range(ends)])  489 us
    dot_general x2, matrix products, attend(): jnp.einsum('qhd,khd->hqk', query_rows, all_keys, preferred_element_type=j...  29.4 us
    dot_general x2, matrix products, attend(): jnp.einsum('hqk,khd->qhd', weights.astype(jnp.bfloat16), all_values, pref...  28.1 us
    reduce_sum x2, other arithmetic, attend(): totals = jnp.sum(weights, axis=-1)  27.5 us
    all_to_all x1, local copies, waits for them, and re-layouts, local(): lax.all_to_all(jnp.stack([prompt_pair] * lax.axis_size('seq')), 'seq', 0, 0)  19.4 us
  transfers between devices with their start and end apart: 3, of which 1 were waited for; matrix products, arithmetic and copies ran while one was open for 8% of the time, Pallas kernels for 0%

profile of v1, /device:TPU:103, one launch (start us, length us, event | category | flops | bytes accessed | tf_op | source)
XLA Modules:
  0.0 739.5 jit_solution(1515073427101441310)
XLA Ops:
  1.1 7.9 %stack.33 = bf16[32,2,32,8,640]{4,3,2,1,0:T(8,128)(2,1)} broadcast(bf16[2,32,8,640]{3,2,1,0:T(8,128)(2,1)S(1)} %pad_maximum_fusion.4), dimensions={1,2,3,4} | broadcast | bytes 21626880 | tf_op jit(solution)/shard_map/stack | solution.py:114
  9.1 10.0 %all-to-all-start = ((bf16[32,2,32,8,640]{4,3,2,1,0:T(8,128)(2,1)}), bf16[32,2,32,8,640]{4,3,2,1,0:T(8,128)(2,1)}, u32[]{:S(2)}, u32[]{:S(2)}) async-start(bf16[32,2,32,8,640]{4,3,2,1,0:T(8,128)(2,1)} %stack.33), calls=%async_computation | async-start | bytes 41943040 | tf_op jit(solution)/shard_map/all_to_all | solution.py:114
  19.8 13.8 %all-reduce = (f32[1024]{0:T(1024)S(1)}, f32[1024]{0:T(1024)S(1)}) all-reduce(f32[1024]{0:T(1024)S(1)} %fusion.26, f32[1024]{0:T(1024)S(1)} %fusion.28), channel_id=1, replica_groups=mesh['seq'=32,'head'=8] {'head'}, use_global_device_ids=true, to_apply=%region_8.9 | all-reduce | flops 2048 | bytes 16384 | tf_op jit(solution)/shard_map/psum | solution.py:104
  37.4 4.4 reshape_reshape.8
  45.6 4.6 reshape_reshape.9
  52.5 9.1 %subtract_convert_fusion = (bf16[1024,5,64,1]{0,3,2,1:T(2,128)(2,1)}, bf16[1024,5,64,1]{0,3,2,1:T(2,128)(2,1)}, bf16[1024,5,64,1]{0,3,2,1:T(2,128)(2,1)S(1)}, bf16[1024,5,64,1]{0,3,2,1:T(2,128)(2,1)S(1)}) fusion(f32[1024,5,64,2]{0,3,2,1:T(2,128)} %reshape_reshape.9, f32[1024,64]{0,1:T(8,128)S(1)} %get-tuple-element.201, ...), kind=kLoop, calls=%fused_computation.47 | loop fusion | flops 5242880 | bytes 8388608 | tf_op jit(solution)/shard_map/convert.2
  69.2 4.3 collective-permute-start
  75.7 5.8 pad_maximum_fusion.3
  81.4 4.1 convert_element_type.86
  89.4 488.9 %collective-permute-done = bf16[2,896,640]{1,2,0:T(8,128)(2,1)} collective-permute-done((bf16[2,896,640]{1,2,0:T(8,128)(2,1)}, bf16[2,896,640]{1,2,0:T(8,128)(2,1)}, u32[]{:S(2)}, u32[]{:S(2)}) %collective-permute-start) | collective-permute-done | bytes 2293792 | tf_op jit(solution)/shard_map/ppermute | solution.py:23
  578.3 5.7 pad_maximum_fusion
  584.0 19.4 %copy.66 = bf16[32,2,32,8,640]{4,3,0,2,1:T(8,128)(2,1)} copy(bf16[32,2,32,8,640]{4,3,2,1,0:T(8,128)(2,1)} %all-to-all-done) | data formatting | bytes 41943040 | tf_op jit(solution)/shard_map/all_to_all | solution.py:114
  603.4 7.7 %gather_fusion = bf16[2,2,256,640]{3,2,1,0:T(8,128)(2,1)S(1)} fusion(bf16[2,32,256,640]{3,2,1,0:T(8,128)(2,1)} %bitcast.121, s32[1024]{0:T(1024)S(1)} %pad_clamp_fusion), kind=kCustom, calls=%fused_computation | custom fusion | bytes 2621448 | tf_op jit(solution)/shard_map/jit(_take)/gather | solution.py:117
  615.4 124.1 %while.12 = (s32[]{:T(128)}, bf16[2,512,640]{2,1,0:T(8,128)(2,1)}, bf16[2,2816,640]{1,2,0:T(8,128)(2,1)}, s32[2]{0:T(128)S(1)}, bf16[512,5,128]{0,2,1:T(8,128)(2...) while((s32[]{:T(128)}, bf16[2,512,640]{2,1,0:T(8,128)(2,1)}, ...), condition=%wide.region_14.15_spmd, body=%wide.region_11.14_spmd.sunk | while | flops 3786796032 | bytes 151642208 | solution.py:172
  623.6 3.6 fusion.54
  629.3 3.3 copy.75
  633.8 14.7 %fusion.55 = (f32[5,512]{1,0:T(8,128)S(1)}, f32[5,512,2816]{2,1,0:T(8,128)}) fusion(pred[512,2816]{1,0:T(8,128)(4,1)} %copy.74, bf16[512,5,128]{0,2,1:T(8,128)(2,1)S(1)} %bitcast.123, bf16[512,5,128]{2,0,1:T(8,128)(2,1)} %get-tuple-element.322, bf16[2304,5,128]{2,0,1:T(8,128)(2,1)} %copy.75), kind=kOutput, calls=%fused_computation.3.clone.1 | convolution fusion | flops 1874327040 | bytes 34547712 | tf_op jit(solution)/shard_map/while/body/eval_jaxpr/qhd,khd->hqk/dot_general | solution.py:156
  648.5 13.8 %fusion.56 = f32[5,512]{1,0:T(8,128)S(1)} fusion(f32[5,512,2816]{2,1,0:T(8,128)} %get-tuple-element.275, f32[5,512]{1,0:T(8,128)S(1)} %get-tuple-element.276, pred[512,2816]{1,0:T(8,128)(4,1)S(1)} %copy-done), kind=kLoop, calls=%fused_computation.4.clone.1 | loop fusion | flops 28833280 | bytes 30298112 | tf_op jit(solution)/shard_map/while/body/eval_jaxpr/reduce_sum | solution.py:162
  662.2 14.0 %divide_convert_fusion.2 = bf16[512,5,128]{0,2,1:T(8,128)(2,1)S(1)} fusion(f32[512,5]{0,1:T(8,128)S(1)} %bitcast.128, f32[5,512,2816]{2,1,0:T(8,128)} %get-tuple-element.275, f32[5,512]{1,0:T(8,128)S(1)} %get-tuple-element.276, pred[512,2816]{1,0:T(8,128)(4,1)S(1)} %copy-done, bf16[512,5,128]{0,2,1:T(8,128)(2,1)S(1)} %copy-done.4, ...), kind=kOutput, calls=%fused_computation.17.clone.1 | convolution fusion | flops 1882193920 | bytes 34557952 | tf_op jit(solution)/shard_map/while/body/eval_jaxpr/hqk,khd->qhd/dot_general | solution.py:163
  685.7 3.6 fusion.54
  691.4 3.3 copy.75
  695.8 14.7 %fusion.55 = (f32[5,512]{1,0:T(8,128)S(1)}, f32[5,512,2816]{2,1,0:T(8,128)}) fusion(pred[512,2816]{1,0:T(8,128)(4,1)} %copy.74, bf16[512,5,128]{0,2,1:T(8,128)(2,1)S(1)} %bitcast.123, bf16[512,5,128]{2,0,1:T(8,128)(2,1)} %get-tuple-element.322, bf16[2304,5,128]{2,0,1:T(8,128)(2,1)} %copy.75), kind=kOutput, calls=%fused_computation.3.clone.1 | convolution fusion | flops 1874327040 | bytes 34547712 | tf_op jit(solution)/shard_map/while/body/eval_jaxpr/qhd,khd->hqk/dot_general | solution.py:156
  710.5 13.8 %fusion.56 = f32[5,512]{1,0:T(8,128)S(1)} fusion(f32[5,512,2816]{2,1,0:T(8,128)} %get-tuple-element.275, f32[5,512]{1,0:T(8,128)S(1)} %get-tuple-element.276, pred[512,2816]{1,0:T(8,128)(4,1)S(1)} %copy-done), kind=kLoop, calls=%fused_computation.4.clone.1 | loop fusion | flops 28833280 | bytes 30298112 | tf_op jit(solution)/shard_map/while/body/eval_jaxpr/reduce_sum | solution.py:162
  724.3 14.0 %divide_convert_fusion.2 = bf16[512,5,128]{0,2,1:T(8,128)(2,1)S(1)} fusion(f32[512,5]{0,1:T(8,128)S(1)} %bitcast.128, f32[5,512,2816]{2,1,0:T(8,128)} %get-tuple-element.275, f32[5,512]{1,0:T(8,128)S(1)} %get-tuple-element.276, pred[512,2816]{1,0:T(8,128)(4,1)S(1)} %copy-done, bf16[512,5,128]{0,2,1:T(8,128)(2,1)S(1)} %copy-done.4, ...), kind=kOutput, calls=%fused_computation.17.clone.1 | convolution fusion | flops 1882193920 | bytes 34557952 | tf_op jit(solution)/shard_map/while/body/eval_jaxpr/hqk,khd->qhd/dot_general | solution.py:163
  (105 shorter events, 51.7 us)
Async XLA Ops:
  9.1 10.0 %copy-start.2 = (bf16[1024,640]{1,0:T(8,128)(2,1)S(1)}, bf16[1024,640]{1,0:T(8,128)(2,1)}, u32[]{:S(2)}) copy-start(bf16[1024,640]{1,0:T(8,128)(2,1)} %param.13) | copy-start | bytes 3932164
  9.1 10.4 %copy-start.3 = (bf16[1024,640]{1,0:T(8,128)(2,1)S(1)}, bf16[1024,640]{1,0:T(8,128)(2,1)}, u32[]{:S(2)}) copy-start(bf16[1024,640]{1,0:T(8,128)(2,1)} %param.12) | copy-start | bytes 3932164
  9.1 575.0 %all-to-all-start = ((bf16[32,2,32,8,640]{4,3,2,1,0:T(8,128)(2,1)}), bf16[32,2,32,8,640]{4,3,2,1,0:T(8,128)(2,1)}, u32[]{:S(2)}, u32[]{:S(2)}) async-start(bf16[32,2,32,8,640]{4,3,2,1,0:T(8,128)(2,1)} %stack.33), calls=%async_computation | async-start | bytes 41943040 | tf_op jit(solution)/shard_map/all_to_all | solution.py:114
  19.1 14.5 %copy-start.7 = (f32[640]{0:T(1024)S(1)}, f32[640]{0:T(1024)}, u32[]{:S(2)}) copy-start(f32[640]{0:T(1024)} %param.16) | copy-start | bytes 7684
  37.4 4.5 copy-start.8
  45.6 4.6 copy-start.5
  45.6 5.0 copy-start.9
  45.6 7.0 copy-start.1
  69.2 509.1 %collective-permute-start = (bf16[2,896,640]{1,2,0:T(8,128)(2,1)}, bf16[2,896,640]{1,2,0:T(8,128)(2,1)}, u32[]{:S(2)}, u32[]{:S(2)}) collective-permute-start(bf16[2,896,640]{1,2,0:T(8,128)(2,1)} %get-tuple-element.194), channel_id=1, source_target_pairs={{0,8},{8,16},{16,24},{24,32},{32,40},{40,48},{48,56},{56,64},{64,7... | collective-permute-start | bytes 6881288 | tf_op jit(solution)/shard_map/ppermute | solution.py:23
  73.5 504.8 %collective-permute-start.1 = (bf16[2,896,640]{1,2,0:T(8,128)(2,1)}, bf16[2,896,640]{1,2,0:T(8,128)(2,1)}, u32[]{:S(2)}, u32[]{:S(2)}) collective-permute-start(bf16[2,896,640]{1,2,0:T(8,128)(2,1)} %get-tuple-element.195), channel_id=1, source_target_pairs={{8,0},{16,8},{24,16},{32,24},{40,32},{48,40},{56,48},{64,56},{72,6... | collective-permute-start | bytes 6881288 | tf_op jit(solution)/shard_map/ppermute | solution.py:25
  75.6 12.9 %copy-start.6 = (s32[8,27]{1,0:T(8,128)S(1)}, s32[8,27]{1,0:T(8,128)}, u32[]{:S(2)}) copy-start(s32[8,27]{1,0:T(8,128)} %param.18) | copy-start | bytes 2596
  633.8 14.7 %copy-start = (pred[512,2816]{1,0:T(8,128)(4,1)S(1)}, pred[512,2816]{1,0:T(8,128)(4,1)}, u32[]{:S(2)}) copy-start(pred[512,2816]{1,0:T(8,128)(4,1)} %copy.74) | copy-start | bytes 4325380 | tf_op jit(solution)/shard_map/while
  648.5 13.8 %copy-start.4 = (bf16[512,5,128]{0,2,1:T(8,128)(2,1)S(1)}, bf16[512,5,128]{0,2,1:T(8,128)(2,1)}, u32[]{:S(2)}) copy-start(bf16[512,5,128]{0,2,1:T(8,128)(2,1)} %get-tuple-element.318) | copy-start | bytes 1966084 | tf_op jit(solution)/shard_map/while
  695.8 14.7 %copy-start = (pred[512,2816]{1,0:T(8,128)(4,1)S(1)}, pred[512,2816]{1,0:T(8,128)(4,1)}, u32[]{:S(2)}) copy-start(pred[512,2816]{1,0:T(8,128)(4,1)} %copy.74) | copy-start | bytes 4325380 | tf_op jit(solution)/shard_map/while
  710.5 13.8 %copy-start.4 = (bf16[512,5,128]{0,2,1:T(8,128)(2,1)S(1)}, bf16[512,5,128]{0,2,1:T(8,128)(2,1)}, u32[]{:S(2)}) copy-start(bf16[512,5,128]{0,2,1:T(8,128)(2,1)} %get-tuple-element.318) | copy-start | bytes 1966084 | tf_op jit(solution)/shard_map/while
